TPU v7x, 256 devices: a whole 4x4x8 slice. The times are simulated.
256 devices in a mesh: user: 16 (over z, core), item: 16 (over y, x).
Axes of the slice: x: 4, y: 4, z: 8, core: 2. Of those that a mesh axis runs over, the one named last changes fastest.
Arguments:
- user_factors: float32 [8192, 256], P('user'), may hold values from -0.3 to 0.3, as said below
- item_factors: float32 [8192, 256], P('item'), may hold values from -0.6 to 0.6
- tile_user: int32 [16, 16, 16, 2], P('item', 'user'), may hold values from 0 to 3
- tile_item: int32 [16, 16, 16, 2], P('item', 'user'), may hold values from 0 to 3
- tile_count: int32 [16, 16, 16], P('item', 'user'), may hold values from 1 to 2, as said below
- tile_conf: bfloat16 [16, 16, 16, 2, 128, 128], P('item', 'user'), may hold values from 0.099609375 to 4
- held_user: int32 [16, 16, 16, 2], P('user', 'item'), may hold values from 0 to 1
- held_item: int32 [16, 16, 16, 2], P('user', 'item'), may hold values from 0 to 3
- held_count: int32 [16, 16, 16], P('user', 'item'), may hold values from 1 to 2, as said below
- held_conf: bfloat16 [16, 16, 16, 2, 128, 128], P('user', 'item'), may hold values from 0.099609375 to 4
Outputs:
- new_items: float32 [8192, 256], P('item')
- folded_users: float32 [4096, 256], P('user')
Inputs may be any that keep to these rules, and one draw needn't show every extreme that they name: `user_factors`: user factors; the scale of a factor column varies by up to a factor of ten. `tile_count`: some device has an owner with all 2 slots live and one with a single live slot. `held_count`: some device has an owner with all 2 slots live and one with a single live slot.
All inputs are finite; a program needn't handle non-finite values.
Results may differ from a plain program's by a relative error of at most 0.0003.
Values may be sent and summed in bfloat16 or wider, within the bound.
No kernel may reach another device: no remote copies, remote signals or barrier semaphores. Data moves between devices by JAX's collectives and lax.ppermute only.
A program may use at most 128 MiB of HBM per device.

v0:
```python
import jax
import jax.numpy as jnp
from jax import lax
from jax.sharding import PartitionSpec as P

HB_DEV = 2
ITERS = 2
highest = lax.Precision.HIGHEST
ridge_weight = 1.0
epsilon = 1e-06


def local_gram(rows):
    return jnp.einsum("nk,nm->km", rows, rows, precision=highest)


def gram_apply(vector, gram):
    return jnp.einsum("jck,km->jcm", vector, gram, precision=highest) + ridge_weight * vector


def block_onehot(positions, blocks):
    return (positions[:, None] == jnp.arange(blocks, dtype=jnp.int32)[None, :]).astype(jnp.float32)


def item_terms(factors, weights, positions, onehot, vector):
    picked = vector[positions]
    scores = jnp.einsum("tuk,tik->tui", factors, picked, precision=highest) * weights
    terms = jnp.einsum("tui,tuk->tik", scores, factors, precision=highest)
    return jnp.einsum("tj,tik->jik", onehot, terms, precision=highest)


def item_right(factors, right_weights, onehot):
    terms = jnp.einsum("tui,tuk->tik", right_weights, factors, precision=highest)
    return jnp.einsum("tj,tik->jik", onehot, terms, precision=highest)


def held_terms(factors, weights, positions, onehot, vector):
    picked = vector[positions]
    scores = jnp.einsum("tik,thk->thi", factors, picked, precision=highest) * weights
    terms = jnp.einsum("thi,tik->thk", scores, factors, precision=highest)
    return jnp.einsum("tj,thk->jhk", onehot, terms, precision=highest)


def held_right(factors, right_weights, onehot):
    terms = jnp.einsum("thi,tik->thk", right_weights, factors, precision=highest)
    return jnp.einsum("tj,thk->jhk", onehot, terms, precision=highest)


def conjugate(operator, residual, start):
    solution = start
    direction = residual
    norm_now = jnp.sum(residual * residual, axis=-1, keepdims=True)
    for iteration in range(ITERS):
        image = operator(direction)
        alpha = norm_now / (jnp.sum(direction * image, axis=-1, keepdims=True) + epsilon)
        solution = solution + alpha * direction
        residual = residual - alpha * image
        norm_next = jnp.sum(residual * residual, axis=-1, keepdims=True)
        direction = residual + norm_next / (norm_now + epsilon) * direction
        norm_now = norm_next
    return solution


def user_total(partial_value):
    return lax.psum(partial_value, "user")


def item_total(partial_value):
    return lax.psum(partial_value, "item")


def tile_weights(confidence, live_slots, tile_width):
    live_flat = live_slots.reshape(-1).astype(jnp.float32)[:, None, None]
    conf_flat = confidence.reshape(-1, tile_width, tile_width).astype(jnp.float32)
    return (conf_flat * live_flat, (1.0 + conf_flat) * live_flat)


def shards(
    user_factors,
    item_factors,
    tile_user,
    tile_item,
    tile_count,
    tile_conf,
    held_user,
    held_item,
    held_count,
    held_conf,
):
    factor_rank = user_factors.shape[1]
    tile_width = tile_conf.shape[-1]
    user_peers = lax.axis_size("user")
    item_peers = lax.axis_size("item")
    user_index = tile_user[0, 0]
    item_index = tile_item[0, 0]
    slot_count = user_index.shape[1]
    live_slots = (
        jnp.arange(slot_count, dtype=jnp.int32)[None, :] < tile_count[0, 0][:, None]
    ).astype(jnp.int32)
    confidence = tile_conf[0, 0]
    whole_users = lax.all_gather(user_factors, "user", axis=0, tiled=True)
    gram_users = lax.psum(local_gram(user_factors), "user")
    user_table = whole_users.reshape(user_peers, -1, tile_width, factor_rank)
    tile_factors = user_table[jnp.arange(user_peers, dtype=jnp.int32)[:, None], user_index]
    factors = tile_factors.reshape(-1, tile_width, factor_rank)
    weights, right_weights = tile_weights(confidence, live_slots, tile_width)
    item_blocks = item_factors.shape[0] // tile_width
    positions = item_index.reshape(-1)
    onehot = block_onehot(positions, item_blocks)
    warm_start = item_factors.reshape(item_blocks, tile_width, factor_rank)

    def item_operator(direction):
        return user_total(item_terms(factors, weights, positions, onehot, direction)) + gram_apply(
            direction, gram_users
        )

    start_total = user_total(
        item_right(factors, right_weights, onehot)
        - item_terms(factors, weights, positions, onehot, warm_start)
    )
    residual = start_total - gram_apply(warm_start, gram_users)
    own_items = conjugate(item_operator, residual, warm_start)
    new_items = own_items.reshape(-1, factor_rank)
    held_index = held_user[0, 0]
    owner_index = held_item[0, 0]
    held_slots = owner_index.shape[1]
    held_live = (
        jnp.arange(held_slots, dtype=jnp.int32)[None, :] < held_count[0, 0][:, None]
    ).astype(jnp.int32)
    held_confidence = held_conf[0, 0]
    whole_items = lax.all_gather(new_items, "item", axis=0, tiled=True)
    gram_items = lax.psum(local_gram(new_items), "item")
    item_table = whole_items.reshape(item_peers, -1, tile_width, factor_rank)
    held_factors = item_table[jnp.arange(item_peers, dtype=jnp.int32)[:, None], owner_index]
    held_flat = held_factors.reshape(-1, tile_width, factor_rank)
    held_weights, held_right_weights = tile_weights(held_confidence, held_live, tile_width)
    held_positions = held_index.reshape(-1)
    held_onehot = block_onehot(held_positions, HB_DEV)

    def held_operator(direction):
        return item_total(
            held_terms(held_flat, held_weights, held_positions, held_onehot, direction)
        ) + gram_apply(direction, gram_items)

    held_residual = item_total(held_right(held_flat, held_right_weights, held_onehot))
    zero_start = jnp.zeros((HB_DEV, tile_width, factor_rank), jnp.float32)
    folded_users = conjugate(held_operator, held_residual, zero_start).reshape(-1, factor_rank)
    return (new_items, folded_users)


def solution(mesh):
    in_specs = (
        P("user", None),
        P("item", None),
        P("item", "user", None, None),
        P("item", "user", None, None),
        P("item", "user", None),
        P("item", "user", None, None, None, None),
        P("user", "item", None, None),
        P("user", "item", None, None),
        P("user", "item", None),
        P("user", "item", None, None, None, None),
    )
    out_specs = (P("item", None), P("user", None))
    return jax.shard_map(shards, mesh=mesh, in_specs=in_specs, out_specs=out_specs, check_vma=False)
```

profile of v0, /device:TPU:2, one launch (start us, length us, event | category | flops | bytes accessed | tf_op | source)
XLA Modules:
  0.0 905.1 jit_solution(9983996490653584908)
XLA Ops:
  10.6 3.8 gather_fusion.1
  16.2 52.5 %all-gather.3.cloned.1.call-done = f32[8192,256]{1,0:T(8,128)} async-done(((f32[512,256]{1,0:T(8,128)}), f32[8192,256]{1,0:T(8,128)}) %all-gather.3.cloned.1.call-update) | async-done | bytes 8388624 | tf_op jit(solution)/shard_map/all_gather | solution.py:101
  68.7 6.1 gather_fusion
  74.9 8.0 fusion.80
  82.9 4.5 fusion.30
  87.3 4.7 fusion.23
  92.1 3.8 fusion.10
  95.9 3.8 fusion.12
  101.2 109.1 %all-reduce.19.cloned.1.call-done = (f32[4,128,256]{2,1,0:T(8,128)}, f32[256,256]{1,0:T(8,128)}) async-done(((f32[4,128,256]{2,1,0:T(8,128)}, f32[256,256]{1,0:T(8,128)}), (f32[4,128,256]{2,1,0:T(8,128)}, f32[256,256]{1,0:T(8,128)})) %all-reduce.19.cloned.1.call-update) | async-done | bytes 786448 | tf_op jit(solution)/shard_map/psum | solution.py:65
  214.8 8.0 fusion.82
  222.8 4.5 fusion.25
  227.4 4.0 fusion.8
  232.3 110.0 %all-reduce.9.cloned.1.call-done = f32[4,128,256]{2,1,0:T(8,128)} async-done(((f32[4,128,256]{2,1,0:T(8,128)}), f32[4,128,256]{2,1,0:T(8,128)}) %all-reduce.9.cloned.1.call-update) | async-done | bytes 524304 | tf_op jit(solution)/shard_map/psum | solution.py:65
  344.5 2.8 gather_fusion.3
  347.3 8.0 fusion.83
  355.3 4.5 fusion.27
  359.9 4.0 fusion.6
  364.9 109.9 %all-reduce.11.cloned.1.call-done = f32[4,128,256]{2,1,0:T(8,128)} async-done(((f32[4,128,256]{2,1,0:T(8,128)}), f32[4,128,256]{2,1,0:T(8,128)}) %all-reduce.11.cloned.1.call-update) | async-done | bytes 524304 | tf_op jit(solution)/shard_map/psum | solution.py:65
  478.2 75.8 %all-gather.5.cloned.1.call-done = f32[8192,256]{1,0:T(8,128)} async-done(((f32[512,256]{1,0:T(8,128)}), f32[8192,256]{1,0:T(8,128)}) %all-gather.5.cloned.1.call-update) | async-done | bytes 8388624 | tf_op jit(solution)/shard_map/all_gather | solution.py:131
  554.0 6.2 gather_fusion.4
  560.3 5.6 fusion.33
  565.9 3.8 fusion.4
  572.7 91.6 %all-reduce.13.cloned.1.call-done = f32[2,128,256]{2,1,0:T(8,128)} async-done(((f32[2,128,256]{2,1,0:T(8,128)}), f32[2,128,256]{2,1,0:T(8,128)}) %all-reduce.13.cloned.1.call-update) | async-done | bytes 262160 | tf_op jit(solution)/shard_map/psum | solution.py:69
  664.3 3.7 gather_fusion.5
  668.0 8.0 fusion.84
  676.0 4.5 fusion.19
  680.5 4.0 fusion.2
  685.3 94.8 %all-reduce.17.cloned.1.call-done = (f32[2,128,256]{2,1,0:T(8,128)}, f32[256,256]{1,0:T(8,128)}) async-done(((f32[2,128,256]{2,1,0:T(8,128)}, f32[256,256]{1,0:T(8,128)}), (f32[2,128,256]{2,1,0:T(8,128)}, f32[256,256]{1,0:T(8,128)})) %all-reduce.17.cloned.1.call-update) | async-done | bytes 524304 | tf_op jit(solution)/shard_map/psum | solution.py:69
  784.8 8.0 fusion.85
  792.8 4.5 fusion.21
  797.3 3.8 fusion
  801.9 93.9 %all-reduce.15.cloned.1.call-done = f32[2,128,256]{2,1,0:T(8,128)} async-done(((f32[2,128,256]{2,1,0:T(8,128)}), f32[2,128,256]{2,1,0:T(8,128)}) %all-reduce.15.cloned.1.call-update) | async-done | bytes 262160 | tf_op jit(solution)/shard_map/psum | solution.py:69
  (95 shorter events, 30.0 us)
Async XLA Ops:
  7.2 61.6 %all-gather.3.cloned.1.call-start = ((), (), s32[]{:S(2)}) async-start(), calls=%async_computation | async-start | bytes 8912896 | tf_op jit(solution)/shard_map/all_gather | solution.py:101
  7.9 202.4 %all-reduce.19.cloned.1.call-start = ((), (), s32[]{:S(2)}) async-start(), calls=%async_computation.7 | async-start | bytes 1572864 | tf_op jit(solution)/shard_map/psum | solution.py:65
  10.6 3.9 copy-start.10
  74.9 8.0 copy-start
  74.9 8.0 copy-start.7
  95.9 114.4 %copy-start.6 = (f32[512,256]{1,0:T(8,128)S(1)}, f32[512,256]{1,0:T(8,128)}, u32[]{:S(2)}) copy-start(f32[512,256]{1,0:T(8,128)} %param.11) | copy-start | bytes 1572868
  100.7 241.6 %all-reduce.9.cloned.1.call-start = ((), (), s32[]{:S(2)}) async-start(), calls=%async_computation.1 | async-start | bytes 1048576 | tf_op jit(solution)/shard_map/psum | solution.py:65
  214.8 8.0 copy-start.1
  227.4 114.9 %copy-start.11 = (f32[256,256]{1,0:T(8,128)S(1)}, f32[256,256]{1,0:T(8,128)}, u32[]{:S(2)}) copy-start(f32[256,256]{1,0:T(8,128)} %get-tuple-element.9) | copy-start | bytes 786436
  232.3 242.5 %all-reduce.11.cloned.1.call-start = ((), (), s32[]{:S(2)}) async-start(), calls=%async_computation.2 | async-start | bytes 1048576 | tf_op jit(solution)/shard_map/psum | solution.py:65
  347.3 8.0 copy-start.2
  359.8 117.7 %copy-start.13 = (s32[1,1,16,2]{2,3,1,0:T(2,128)S(1)}, s32[1,1,16,2]{2,3,1,0:T(2,128)}, u32[]{:S(2)}) copy-start(s32[1,1,16,2]{2,3,1,0:T(2,128)} %param.16) | copy-start | bytes 388
  359.9 118.0 %copy-start.14 = (s32[1,1,16,2]{2,3,1,0:T(2,128)S(1)}, s32[1,1,16,2]{2,3,1,0:T(2,128)}, u32[]{:S(2)}) copy-start(s32[1,1,16,2]{2,3,1,0:T(2,128)} %param.17) | copy-start | bytes 388
  359.9 118.2 %copy-start.15 = (s32[1,1,16]{2,1,0:T(1,128)S(1)}, s32[1,1,16]{2,1,0:T(1,128)}, u32[]{:S(2)}) copy-start(s32[1,1,16]{2,1,0:T(1,128)} %param.18) | copy-start | bytes 196
  364.8 189.2 %all-gather.5.cloned.1.call-start = ((), (), s32[]{:S(2)}) async-start(), calls=%async_computation.3 | async-start | bytes 8912896 | tf_op jit(solution)/shard_map/all_gather | solution.py:131
  477.5 186.8 %all-reduce.13.cloned.1.call-start = ((), (), s32[]{:S(2)}) async-start(), calls=%async_computation.4 | async-start | bytes 524288 | tf_op jit(solution)/shard_map/psum | solution.py:69
  554.0 6.2 copy-start.8
  565.9 5.1 copy-start.9
  570.5 209.7 %all-reduce.17.cloned.1.call-start = ((), (), s32[]{:S(2)}) async-start(), calls=%async_computation.6 | async-start | bytes 1048576 | tf_op jit(solution)/shard_map/psum | solution.py:69
  668.0 8.0 copy-start.3
  680.5 99.6 %copy-start.5 = (f32[2,128,256]{2,1,0:T(8,128)S(1)}, f32[2,128,256]{2,1,0:T(8,128)}, u32[]{:S(2)}) copy-start(f32[2,128,256]{2,1,0:T(8,128)} %all-reduce.13.cloned.1.call-done) | copy-start | bytes 786436
  685.3 210.5 %all-reduce.15.cloned.1.call-start = ((), (), s32[]{:S(2)}) async-start(), calls=%async_computation.5 | async-start | bytes 524288 | tf_op jit(solution)/shard_map/psum | solution.py:69
  784.8 8.0 copy-start.4
  797.3 98.5 %copy-start.12 = (f32[256,256]{1,0:T(8,128)S(1)}, f32[256,256]{1,0:T(8,128)}, u32[]{:S(2)}) copy-start(f32[256,256]{1,0:T(8,128)} %get-tuple-element.7) | copy-start | bytes 786436
Sparse Core Ops, SparseCore 0:
  9.8 58.8 all-gather.2
  100.8 109.4 all-reduce.18
  232.4 109.8 all-reduce.8
  364.9 109.7 all-reduce.10
  477.9 76.0 all-gather.4
  570.6 93.7 all-reduce.12
  685.4 94.7 all-reduce.16
  802.0 93.7 all-reduce.14
where the time goes:
time: 914 us; the launch traced here: 905 us
  waiting for transfers between devices  738 us (81%)
  matrix products  112 us (12%)
  local copies, waits for them, and re-layouts  33.9 us (4%)
  between operations  14.7 us (2%)
    psum x3, waiting for transfers between devices, user_total(): return lax.psum(partial_value, 'user')  329 us
    psum x3, waiting for transfers between devices, item_total(): return lax.psum(partial_value, 'item')  280 us
    all_gather x1, waiting for transfers between devices, shards(): whole_items = lax.all_gather(new_items, 'item', axis=0, tiled=True)  75.8 us
    all_gather x1, waiting for transfers between devices, shards(): whole_users = lax.all_gather(user_factors, 'user', axis=0, tiled=True)  52.5 us
    dot_general x3, matrix products, item_terms(): jnp.einsum('tuk,tik->tui', factors, picked, precision=highest) * weights  24 us
  transfers between devices with their start and end apart: 8, of which 8 were waited for; matrix products, arithmetic and copies ran while one was open for 1% of the time, Pallas kernels for 0%

commit v1 on v0

--- a/solution.py
+++ b/solution.py
@@ -8,6 +8,11 @@
 highest = lax.Precision.HIGHEST
 ridge_weight = 1.0
 epsilon = 1e-06
+
+
+def all_by_exchange(array, axis, d):
+    sent = jnp.stack([array] * lax.axis_size(axis))
+    return jnp.concatenate(lax.all_to_all(sent, axis, 0, 0), axis=d)
 
 
 def local_gram(rows):
@@ -98,7 +103,7 @@
         jnp.arange(slot_count, dtype=jnp.int32)[None, :] < tile_count[0, 0][:, None]
     ).astype(jnp.int32)
     confidence = tile_conf[0, 0]
-    whole_users = lax.all_gather(user_factors, "user", axis=0, tiled=True)
+    whole_users = all_by_exchange(user_factors, "user", 0)
     gram_users = lax.psum(local_gram(user_factors), "user")
     user_table = whole_users.reshape(user_peers, -1, tile_width, factor_rank)
     tile_factors = user_table[jnp.arange(user_peers, dtype=jnp.int32)[:, None], user_index]

time: 914 us -> 1050 us (1.15)
  waiting for transfers between devices: 738 us -> 865 us
    all_to_all x0 -> x1, waiting for transfers between devices: none -> 179 us  [all_by_exchange(): return jnp.concatenate(lax.all_to_all(sent, axis, 0, 0), axis=d)]
    all_gather x1 -> x0, waiting for transfers between devices: 52.5 us -> none  [shards(): whole_users = lax.all_gather(user_factors, 'user', axis=0, tiled=True)]
where the time goes in v1:
time: 1050 us; the launch traced here: 1040 us
  waiting for transfers between devices  865 us (82%)
  matrix products  112 us (11%)
  local copies, waits for them, and re-layouts  37.3 us (4%)
  between operations  14.7 us (1%)
    psum x3, waiting for transfers between devices, user_total(): return lax.psum(partial_value, 'user')  330 us
    psum x3, waiting for transfers between devices, item_total(): return lax.psum(partial_value, 'item')  280 us
    all_to_all x1, waiting for transfers between devices, all_by_exchange(): return jnp.concatenate(lax.all_to_all(sent, axis, 0, 0), axis=d)  179 us
    all_gather x1, waiting for transfers between devices, shards(): whole_items = lax.all_gather(new_items, 'item', axis=0, tiled=True)  75.8 us
    dot_general x3, matrix products, item_terms(): jnp.einsum('tuk,tik->tui', factors, picked, precision=highest) * weights  24 us
  transfers between devices with their start and end apart: 8, of which 8 were waited for; matrix products, arithmetic and copies ran while one was open for 1% of the time, Pallas kernels for 0%

profile of v1, /device:TPU:2, one launch (start us, length us, event | category | flops | bytes accessed | tf_op | source)
XLA Modules:
  0.0 1042.6 jit_solution(2107763533154759950)
XLA Ops:
  7.2 5.1 stack.2
  12.3 8.8 all-to-all-start
  26.3 179.0 %all-to-all-done = f32[16,512,256]{2,1,0:T(8,128)} async-done(((f32[16,512,256]{2,1,0:T(8,128)}), f32[16,512,256]{2,1,0:T(8,128)}, u32[]{:S(2)}, u32[]{:S(2)}) %all-to-all-start) | async-done | bytes 8388640 | tf_op jit(solution)/shard_map/all_to_all | solution.py:15
  205.3 6.2 gather_fusion
  211.4 8.0 fusion.80
  219.5 4.5 fusion.30
  223.9 4.7 fusion.23
  228.7 3.8 fusion.10
  232.5 3.8 fusion.12
  237.8 109.8 %all-reduce.19.cloned.1.call-done = (f32[4,128,256]{2,1,0:T(8,128)}, f32[256,256]{1,0:T(8,128)}) async-done(((f32[4,128,256]{2,1,0:T(8,128)}, f32[256,256]{1,0:T(8,128)}), (f32[4,128,256]{2,1,0:T(8,128)}, f32[256,256]{1,0:T(8,128)})) %all-reduce.19.cloned.1.call-update) | async-done | bytes 786448 | tf_op jit(solution)/shard_map/psum | solution.py:70
  352.1 8.0 fusion.82
  360.1 4.5 fusion.25
  364.6 4.0 fusion.8
  369.6 110.0 %all-reduce.9.cloned.1.call-done = f32[4,128,256]{2,1,0:T(8,128)} async-done(((f32[4,128,256]{2,1,0:T(8,128)}), f32[4,128,256]{2,1,0:T(8,128)}) %all-reduce.9.cloned.1.call-update) | async-done | bytes 524304 | tf_op jit(solution)/shard_map/psum | solution.py:70
  484.6 8.0 fusion.83
  492.6 4.5 fusion.27
  497.2 4.0 fusion.6
  502.2 110.1 %all-reduce.11.cloned.1.call-done = f32[4,128,256]{2,1,0:T(8,128)} async-done(((f32[4,128,256]{2,1,0:T(8,128)}), f32[4,128,256]{2,1,0:T(8,128)}) %all-reduce.11.cloned.1.call-update) | async-done | bytes 524304 | tf_op jit(solution)/shard_map/psum | solution.py:70
  615.7 75.8 %all-gather.2.cloned.1.call-done = f32[8192,256]{1,0:T(8,128)} async-done(((f32[512,256]{1,0:T(8,128)}), f32[8192,256]{1,0:T(8,128)}) %all-gather.2.cloned.1.call-update) | async-done | bytes 8388624 | tf_op jit(solution)/shard_map/all_gather | solution.py:136
  691.5 6.3 gather_fusion.4
  697.8 5.6 fusion.33
  703.4 3.8 fusion.4
  710.2 91.6 %all-reduce.13.cloned.1.call-done = f32[2,128,256]{2,1,0:T(8,128)} async-done(((f32[2,128,256]{2,1,0:T(8,128)}), f32[2,128,256]{2,1,0:T(8,128)}) %all-reduce.13.cloned.1.call-update) | async-done | bytes 262160 | tf_op jit(solution)/shard_map/psum | solution.py:74
  801.8 3.7 gather_fusion.5
  805.5 8.0 fusion.84
  813.5 4.5 fusion.19
  818.0 4.0 fusion.2
  822.8 94.8 %all-reduce.17.cloned.1.call-done = (f32[2,128,256]{2,1,0:T(8,128)}, f32[256,256]{1,0:T(8,128)}) async-done(((f32[2,128,256]{2,1,0:T(8,128)}, f32[256,256]{1,0:T(8,128)}), (f32[2,128,256]{2,1,0:T(8,128)}, f32[256,256]{1,0:T(8,128)})) %all-reduce.17.cloned.1.call-update) | async-done | bytes 524304 | tf_op jit(solution)/shard_map/psum | solution.py:74
  922.3 8.0 fusion.85
  930.3 4.5 fusion.21
  934.8 3.8 fusion
  939.4 93.9 %all-reduce.15.cloned.1.call-done = f32[2,128,256]{2,1,0:T(8,128)} async-done(((f32[2,128,256]{2,1,0:T(8,128)}), f32[2,128,256]{2,1,0:T(8,128)}) %all-reduce.15.cloned.1.call-update) | async-done | bytes 262160 | tf_op jit(solution)/shard_map/psum | solution.py:74
  (101 shorter events, 32.8 us)
Async XLA Ops:
  12.2 8.8 copy-start.13
  12.2 9.1 copy-start.15
  12.2 9.3 copy-start.17
  12.3 9.5 copy-start.6
  12.3 193.0 %all-to-all-start = ((f32[16,512,256]{2,1,0:T(8,128)}), f32[16,512,256]{2,1,0:T(8,128)}, u32[]{:S(2)}, u32[]{:S(2)}) async-start(f32[16,512,256]{2,1,0:T(8,128)} %stack.2), calls=%async_computation | async-start | bytes 16777216 | tf_op jit(solution)/shard_map/all_to_all | solution.py:15
  21.0 326.6 %all-reduce.19.cloned.1.call-start = ((), (), s32[]{:S(2)}) async-start(), calls=%async_computation.7 | async-start | bytes 1572864 | tf_op jit(solution)/shard_map/psum | solution.py:70
  21.8 2.8 copy-start.10
  211.4 8.0 copy-start
  211.4 8.0 copy-start.7
  237.3 242.3 %all-reduce.9.cloned.1.call-start = ((), (), s32[]{:S(2)}) async-start(), calls=%async_computation.1 | async-start | bytes 1048576 | tf_op jit(solution)/shard_map/psum | solution.py:70
  352.1 8.0 copy-start.1
  364.6 114.9 %copy-start.11 = (f32[256,256]{1,0:T(8,128)S(1)}, f32[256,256]{1,0:T(8,128)}, u32[]{:S(2)}) copy-start(f32[256,256]{1,0:T(8,128)} %get-tuple-element.9) | copy-start | bytes 786436
  369.5 242.7 %all-reduce.11.cloned.1.call-start = ((), (), s32[]{:S(2)}) async-start(), calls=%async_computation.2 | async-start | bytes 1048576 | tf_op jit(solution)/shard_map/psum | solution.py:70
  484.6 8.0 copy-start.2
  497.1 117.9 %copy-start.14 = (s32[1,1,16,2]{2,3,1,0:T(2,128)S(1)}, s32[1,1,16,2]{2,3,1,0:T(2,128)}, u32[]{:S(2)}) copy-start(s32[1,1,16,2]{2,3,1,0:T(2,128)} %param.16) | copy-start | bytes 388
  497.1 118.2 %copy-start.16 = (s32[1,1,16,2]{2,3,1,0:T(2,128)S(1)}, s32[1,1,16,2]{2,3,1,0:T(2,128)}, u32[]{:S(2)}) copy-start(s32[1,1,16,2]{2,3,1,0:T(2,128)} %param.17) | copy-start | bytes 388
  497.2 118.3 %copy-start.18 = (s32[1,1,16]{2,1,0:T(1,128)S(1)}, s32[1,1,16]{2,1,0:T(1,128)}, u32[]{:S(2)}) copy-start(s32[1,1,16]{2,1,0:T(1,128)} %param.18) | copy-start | bytes 196
  502.1 189.4 %all-gather.2.cloned.1.call-start = ((), (), s32[]{:S(2)}) async-start(), calls=%async_computation.3 | async-start | bytes 8912896 | tf_op jit(solution)/shard_map/all_gather | solution.py:136
  615.0 186.8 %all-reduce.13.cloned.1.call-start = ((), (), s32[]{:S(2)}) async-start(), calls=%async_computation.4 | async-start | bytes 524288 | tf_op jit(solution)/shard_map/psum | solution.py:74
  691.5 6.3 copy-start.8
  703.4 5.1 copy-start.9
  707.9 209.7 %all-reduce.17.cloned.1.call-start = ((), (), s32[]{:S(2)}) async-start(), calls=%async_computation.6 | async-start | bytes 1048576 | tf_op jit(solution)/shard_map/psum | solution.py:74
  805.5 8.0 copy-start.3
  818.0 99.6 %copy-start.5 = (f32[2,128,256]{2,1,0:T(8,128)S(1)}, f32[2,128,256]{2,1,0:T(8,128)}, u32[]{:S(2)}) copy-start(f32[2,128,256]{2,1,0:T(8,128)} %all-reduce.13.cloned.1.call-done) | copy-start | bytes 786436
  822.8 210.5 %all-reduce.15.cloned.1.call-start = ((), (), s32[]{:S(2)}) async-start(), calls=%async_computation.5 | async-start | bytes 524288 | tf_op jit(solution)/shard_map/psum | solution.py:74
  922.3 8.0 copy-start.4
  934.8 98.4 %copy-start.12 = (f32[256,256]{1,0:T(8,128)S(1)}, f32[256,256]{1,0:T(8,128)}, u32[]{:S(2)}) copy-start(f32[256,256]{1,0:T(8,128)} %get-tuple-element.7) | copy-start | bytes 786436
Sparse Core Ops, SparseCore 0:
  237.4 110.1 all-reduce.18
  369.7 109.8 all-reduce.8
  502.2 109.9 all-reduce.10
  615.4 76.0 all-gather.1
  708.1 93.7 all-reduce.12
  822.9 94.7 all-reduce.16
  939.5 93.7 all-reduce.14
